TPU v7x, 256 devices: a whole 4x4x8 slice. The times are simulated.
256 devices in a mesh: row: 8 (over y, core), col: 8 (over x, z_hi), rep: 4 (over z_lo).
Axes of the slice: x: 4, y: 4, z: 8 (z_hi: 2, z_lo: 4; z = z_hi * 4 + z_lo), core: 2. Of those that a mesh axis runs over, the one named last changes fastest.
Arguments:
- features: float32 [256, 32768], P('rep', ('col', 'row')), may hold values from -6 to 6
- weight: float32 [256, 256], replicated, may hold values from -0.375 to 0.375
- cotangent: float32 [256, 32768], P('rep', ('row', 'col')), may hold values from -6 to 6
- tile_values: float32 [10240, 128, 128], P(('row', 'col')), may hold values from -0.078125 to 0.078125
- tile_row: int32 [10240], P(('row', 'col')), may hold values from 0 to 31
- tile_col: int32 [10240], P(('row', 'col')), may hold values from 0 to 31
- tile_kind: int32 [10240], P(('row', 'col')), may hold values from 0 to 159
- tile_count: int32 [64], P(('row', 'col')), may hold values from 40 to 160, as said below
Outputs:
- output: float32 [256, 32768], P('rep', ('row', 'col'))
- input_grad: float32 [256, 32768], P('rep', ('col', 'row'))
- weight_grad: float32 [256, 256], P('rep')
Inputs may be any that keep to these rules, and one draw needn't show every extreme that they name: `tile_count`: a block's slots at or after its count are not part of the adjacency; some block uses all 160 slots. `tile_row`: slots may repeat a tile position; their tiles add. `tile_kind`: an index into the 160 stored tiles of the same block.
All inputs are finite; a program needn't handle non-finite values.
Results may differ from a plain program's by a relative error of at most 0.0001.
Values sent between devices are 32-bit elements; how exact they have to be, the bound alone decides.
No kernel may reach another device: no remote copies, remote signals or barrier semaphores. Data moves between devices by JAX's collectives and lax.ppermute only.
A program may use at most 128 MiB of HBM per device.

v0:
```python
import jax
import jax.numpy as jnp
from jax import lax
from jax.sharding import PartitionSpec as P


def tile_terms(source, values, from_tile, to_tile, tile_kinds, live_weight, dest_tiles, transposed):
    feat_width = source.shape[0]
    tile_edge = values.shape[1]
    tiled = source.reshape(feat_width, source.shape[1] // tile_edge, tile_edge)
    picked = jnp.take(tiled, from_tile, axis=1)
    chosen = jnp.take(values, tile_kinds, axis=0)
    if transposed:
        products = jnp.einsum("fga,gab->fgb", picked, chosen, precision=lax.Precision.HIGHEST)
    else:
        products = jnp.einsum("fgb,gab->fga", picked, chosen, precision=lax.Precision.HIGHEST)
    onehot = (to_tile[:, None] == jnp.arange(dest_tiles, dtype=jnp.int32)[None, :]).astype(
        jnp.float32
    )
    onehot = onehot * live_weight[:, None]
    spread = jnp.einsum("fgt,gd->fdt", products, onehot, precision=lax.Precision.HIGHEST)
    return spread.reshape(feat_width, dest_tiles * tile_edge)


def aggregate(source, values, from_tile, to_tile, tile_kinds, live_count, dest_tiles, transposed):
    slot_total = tile_kinds.shape[0]
    live_weight = (jnp.arange(slot_total, dtype=jnp.int32) < live_count).astype(jnp.float32)
    return tile_terms(
        source, values, from_tile, to_tile, tile_kinds, live_weight, dest_tiles, transposed
    )


def local(features, weight, cotangent, tile_values, tile_row, tile_col, tile_kind, tile_count):
    n_rowdev = lax.axis_size("row")
    n_coldev = lax.axis_size("col")
    n_repdev = lax.axis_size("rep")
    quarter = weight.shape[0] // n_repdev
    rep_index = lax.axis_index("rep")
    own_rows = lax.dynamic_slice_in_dim(weight, rep_index * quarter, quarter, 0)
    own_cols = lax.dynamic_slice_in_dim(weight, rep_index * quarter, quarter, 1)
    stretch_len = features.shape[1]
    tile_edge = tile_values.shape[1]
    live_count = tile_count[0]
    row_tiles = n_coldev * stretch_len // tile_edge
    col_tiles = n_rowdev * stretch_len // tile_edge
    mixed = lax.psum_scatter(
        lax.dot_general(
            own_rows,
            features,
            (((0,), (0,)), ((), ())),
            precision=lax.Precision.HIGHEST,
            preferred_element_type=jnp.float32,
        ),
        "rep",
        scatter_dimension=0,
        tiled=True,
    )
    column_block = lax.all_gather(mixed, "row", axis=1, tiled=True)
    partial_value = aggregate(
        column_block, tile_values, tile_col, tile_row, tile_kind, live_count, row_tiles, False
    )
    summed = lax.psum_scatter(partial_value, "col", scatter_dimension=1, tiled=True)
    output, pullback = jax.vjp(lambda v: jax.nn.gelu(v, approximate=True), summed)
    (grad_pre,) = pullback(cotangent)
    row_block = lax.all_gather(grad_pre, "col", axis=1, tiled=True)
    partial_back = aggregate(
        row_block, tile_values, tile_row, tile_col, tile_kind, live_count, col_tiles, True
    )
    grad_mixed = lax.psum_scatter(partial_back, "row", scatter_dimension=1, tiled=True)
    input_grad = lax.psum_scatter(
        jnp.dot(
            own_cols,
            grad_mixed,
            preferred_element_type=jnp.float32,
            precision=lax.Precision.HIGHEST,
        ),
        "rep",
        scatter_dimension=0,
        tiled=True,
    )
    weight_part = lax.dot_general(
        features,
        lax.all_gather(grad_mixed, "rep", axis=0, tiled=True),
        (((1,), (1,)), ((), ())),
        precision=lax.Precision.HIGHEST,
        preferred_element_type=jnp.float32,
    )
    node_total = stretch_len * n_rowdev * n_coldev
    weight_grad = lax.psum(weight_part * float(node_total) ** (-0.5), ("row", "col"))
    return (output, input_grad, weight_grad)


def solution(mesh):
    return jax.shard_map(
        local,
        mesh=mesh,
        in_specs=(
            P("rep", ("col", "row")),
            P(),
            P("rep", ("row", "col")),
            P(("row", "col"), None, None),
            P(("row", "col")),
            P(("row", "col")),
            P(("row", "col")),
            P(("row", "col")),
        ),
        out_specs=(P("rep", ("row", "col")), P("rep", ("col", "row")), P("rep", None)),
        check_vma=False,
    )
```

profile of v0, /device:TPU:2, one launch (start us, length us, event | category | flops | bytes accessed | tf_op | source)
XLA Modules:
  0.0 1082.4 jit_solution(2901445615518222513)
XLA Ops:
  7.2 0.9 copy-done
  8.1 2.3 fusion.39
  10.5 0.0 all-gather.3.cloned.1.call-start
  10.5 30.2 %reduce-scatter.5.cloned.1.call-done = f32[64,512]{1,0:T(8,128)} async-done(((f32[256,512]{1,0:T(8,128)}), f32[64,512]{1,0:T(8,128)}) %reduce-scatter.5.cloned.1.call-update) | async-done | bytes 131088 | tf_op jit(solution)/shard_map/reduce_scatter | solution.py:46
  40.7 0.0 reduce-scatter.7.cloned.1.call-start
  41.4 0.7 compare_select_fusion.2
  42.1 14.2 %gather_fusion = f32[160,128,128]{2,1,0:T(8,128)} fusion(f32[160,128,128]{2,1,0:T(8,128)} %param.15, s32[1024]{0:T(1024)S(1)} %pad_clamp_fusion.2), kind=kCustom, calls=%fused_computation.clone | custom fusion | bytes 20972160 | tf_op jit(solution)/shard_map/jit(_take)/gather | solution.py:12
  56.3 10.5 all-gather.3.cloned.1.call-done
  66.8 1.3 copy_bitcast_fusion.3
  68.2 3.3 gather_fusion.1
  71.5 24.3 %fusion.20 = f32[64,160,128]{2,0,1:T(8,128)S(1)} fusion(f32[160,64,128]{2,1,0:T(8,128)} %gather_fusion.1, pred[160]{0:T(512)(128)(4,1)S(1)} %get-tuple-element.7, f32[160,128,128]{2,1,0:T(8,128)} %gather_fusion, pred[160]{0:T(512)(128)(4,1)S(1)} %get-tuple-element.8), kind=kOutput, calls=%fused_computation.23 | convolution fusion | flops 2017198080 | bytes 20971840 | tf_op jit(solution)/shard_map/fgb,gab->fga/dot_general | solution.py:16
  95.8 5.6 fusion.8
  101.5 1.6 copy.29
  103.1 0.0 all-gather.5.cloned.1.call-start
  103.1 87.2 %reduce-scatter.7.cloned.1.call-done = f32[64,512]{1,0:T(8,128)} async-done(((f32[64,4096]{1,0:T(8,128)}), f32[64,512]{1,0:T(8,128)}) %reduce-scatter.7.cloned.1.call-update) | async-done | bytes 131088 | tf_op jit(solution)/shard_map/reduce_scatter | solution.py:62
  190.4 1.7 fusion.36
  192.1 0.0 reduce-scatter.9.cloned.1.call-start
  192.2 59.1 %all-gather.5.cloned.1.call-done = f32[64,4096]{1,0:T(8,128)} async-done(((f32[64,512]{1,0:T(8,128)}), f32[64,4096]{1,0:T(8,128)}) %all-gather.5.cloned.1.call-update) | async-done | bytes 1048592 | tf_op jit(solution)/shard_map/all_gather | solution.py:65
  251.3 1.3 copy_bitcast_fusion.2
  252.7 3.3 gather_fusion.2
  255.9 13.9 %fusion.25 = f32[64,160,128]{2,0,1:T(8,128)S(1)} fusion(f32[160,64,128]{2,1,0:T(8,128)} %gather_fusion.2, pred[160]{0:T(512)(128)(4,1)S(1)} %compare_and_fusion, f32[160,128,128]{2,1,0:T(8,128)} %gather_fusion, pred[160]{0:T(512)(128)(4,1)S(1)} %get-tuple-element.8), kind=kOutput, calls=%fused_computation.24 | convolution fusion | flops 2017198080 | bytes 20971840 | tf_op jit(solution)/shard_map/fga,gab->fgb/dot_general | solution.py:14
  269.8 5.6 fusion.6
  275.5 1.6 copy.28
  277.1 0.0 all-reduce.2.cloned.1.call-start
  277.1 30.8 %reduce-scatter.9.cloned.1.call-done = f32[64,512]{1,0:T(8,128)} async-done(((f32[64,4096]{1,0:T(8,128)}), f32[64,512]{1,0:T(8,128)}) %reduce-scatter.9.cloned.1.call-update) | async-done | bytes 131088 | tf_op jit(solution)/shard_map/reduce_scatter | solution.py:69
  307.9 16.4 %all_gather.11 = f32[256,512]{1,0:T(8,128)S(1)} all-gather(f32[64,512]{1,0:T(8,128)} %reduce-scatter.9.cloned.1.call-done), channel_id=1, replica_groups=mesh['row'=8,'col'=8,'rep'=4] {'rep'}, dimensions={0}, use_global_device_ids=true | all-gather | bytes 655360 | tf_op jit(solution)/shard_map/all_gather | solution.py:83
  324.4 1.2 fusion.30
  325.6 0.0 reduce-scatter.11.cloned.1.call-start
  325.7 2.3 fusion.37
  328.0 722.2 %all-reduce.2.cloned.1.call-done = f32[64,256]{1,0:T(8,128)} async-done(((f32[64,256]{1,0:T(8,128)}), f32[64,256]{1,0:T(8,128)}) %all-reduce.2.cloned.1.call-update) | async-done | bytes 65552 | tf_op jit(solution)/shard_map/psum | solution.py:89
  1050.2 23.9 %reduce-scatter.11.cloned.1.call-done = f32[64,512]{1,0:T(8,128)} async-done(((f32[256,512]{1,0:T(8,128)}), f32[64,512]{1,0:T(8,128)}) %reduce-scatter.11.cloned.1.call-update) | async-done | bytes 131088 | tf_op jit(solution)/shard_map/reduce_scatter | solution.py:70
  1074.1 1.5 copy.32
  (27 shorter events, 0.2 us)
Async XLA Ops:
  7.2 1.0 copy-start
  7.2 33.5 %reduce-scatter.5.cloned.1.call-start = ((), (), s32[]{:S(2)}) async-start(), calls=%async_computation.4 | async-start | bytes 655360 | tf_op jit(solution)/shard_map/reduce_scatter | solution.py:46
  10.5 56.4 %all-gather.3.cloned.1.call-start = ((), (), s32[]{:S(2)}) async-start(), calls=%async_computation.5 | async-start | bytes 1179648 | tf_op jit(solution)/shard_map/all_gather | solution.py:58
  40.7 149.7 %reduce-scatter.7.cloned.1.call-start = ((), (), s32[]{:S(2)}) async-start(), calls=%async_computation.6 | async-start | bytes 1179648 | tf_op jit(solution)/shard_map/reduce_scatter | solution.py:62
  42.1 14.2 %copy-start.3 = (s32[160]{0:T(256)S(1)}, s32[160]{0:T(256)}, u32[]{:S(2)}) copy-start(s32[160]{0:T(256)} %param.17) | copy-start | bytes 1924
  42.1 14.2 %copy-start.5 = (s32[160]{0:T(256)S(1)}, s32[160]{0:T(256)}, u32[]{:S(2)}) copy-start(s32[160]{0:T(256)} %param.18) | copy-start | bytes 1924
  71.5 24.3 %copy-start.4 = (s32[160]{0:T(256)S(1)}, s32[160]{0:T(256)}, u32[]{:S(2)}) copy-start(s32[160]{0:T(256)} %param.16) | copy-start | bytes 1924
  95.8 94.6 %copy-start.2 = (f32[64,512]{1,0:T(8,128)S(1)}, f32[64,512]{1,0:T(8,128)}, u32[]{:S(2)}) copy-start(f32[64,512]{1,0:T(8,128)} %param.14) | copy-start | bytes 393220
  103.1 148.2 %all-gather.5.cloned.1.call-start = ((), (), s32[]{:S(2)}) async-start(), calls=%async_computation.7 | async-start | bytes 1179648 | tf_op jit(solution)/shard_map/all_gather | solution.py:65
  192.1 115.8 %reduce-scatter.9.cloned.1.call-start = ((), (), s32[]{:S(2)}) async-start(), calls=%async_computation.8 | async-start | bytes 1179648 | tf_op jit(solution)/shard_map/reduce_scatter | solution.py:69
  269.8 54.5 %copy-start.1 = (f32[64,512]{1,0:T(8,128)S(1)}, f32[64,512]{1,0:T(8,128)}, u32[]{:S(2)}) copy-start(f32[64,512]{1,0:T(8,128)} %param.12) | copy-start | bytes 393220
  277.1 773.1 %all-reduce.2.cloned.1.call-start = ((), (), s32[]{:S(2)}) async-start(), calls=%async_computation.10 | async-start | bytes 131072 | tf_op jit(solution)/shard_map/psum | solution.py:89
  325.6 748.5 %reduce-scatter.11.cloned.1.call-start = ((), (), s32[]{:S(2)}) async-start(), calls=%async_computation.9 | async-start | bytes 655360 | tf_op jit(solution)/shard_map/reduce_scatter | solution.py:70
Sparse Core Ops, SparseCore 0:
  10.6 30.0 reduce-scatter.4
  42.5 24.2 all-gather.2
  103.2 87.1 reduce-scatter.6
  193.4 57.8 all-gather.4
  277.2 30.6 reduce-scatter.8
  325.7 724.4 all-reduce.1
  1053.3 20.7 reduce-scatter.10
where the time goes:
time: 1080 us
  waiting for transfers between devices  964 us (89%)
  matrix products  55.3 us (5%)
  local copies, waits for them, and re-layouts  29 us (3%)
  blocking collectives  16.4 us (2%)
  between operations  14.9 us (1%)
    psum x1, waiting for transfers between devices, local(): lax.psum(weight_part * float(node_total) ** (-0.5), ('row', 'col'))  722 us
    reduce_scatter x1, waiting for transfers between devices, local(): lax.psum_scatter(partial_value, 'col', scatter_dimension=1, tiled=True)  87.2 us
    all_gather x1, waiting for transfers between devices, local(): row_block = lax.all_gather(grad_pre, 'col', axis=1, tiled=True)  59.1 us
    reduce_scatter x1, waiting for transfers between devices, local(): lax.psum_scatter(partial_back, 'row', scatter_dimension=1, tiled=True)  30.8 us
    reduce_scatter x1, waiting for transfers between devices, local(): lax.psum_scatter(lax.dot_general(own_rows, features, (((0,), (0,)), ((),...  30.2 us
    dot_general x1, matrix products, tile_terms(): jnp.einsum('fgb,gab->fga', picked, chosen, precision=lax.Precision.HIGHEST)  24.3 us
    reduce_scatter x1, waiting for transfers between devices, local(): lax.psum_scatter(jnp.dot(own_cols, grad_mixed, preferred_element_type=jnp...  23.9 us
  transfers between devices with their start and end apart: 7, of which 7 were waited for; matrix products, arithmetic and copies ran while one was open for 2% of the time, Pallas kernels for 0%

commit v1 on v0

--- a/solution.py
+++ b/solution.py
@@ -62,7 +62,10 @@
     summed = lax.psum_scatter(partial_value, "col", scatter_dimension=1, tiled=True)
     output, pullback = jax.vjp(lambda v: jax.nn.gelu(v, approximate=True), summed)
     (grad_pre,) = pullback(cotangent)
-    row_block = lax.all_gather(grad_pre, "col", axis=1, tiled=True)
+    n_dev = lax.axis_size("col")
+    blocks = jnp.stack([grad_pre for _ in range(n_dev)])
+    blocks = lax.all_to_all(blocks, "col", split_axis=0, concat_axis=0)
+    row_block = jnp.concatenate(blocks, axis=1)
     partial_back = aggregate(
         row_block, tile_values, tile_row, tile_col, tile_kind, live_count, col_tiles, True
     )

time: 1080 us -> 1060 us (0.981)
  waiting for transfers between devices: 964 us -> 934 us
    all_gather x1 -> x0, waiting for transfers between devices: 59.1 us -> none  [local(): row_block = lax.all_gather(grad_pre, 'col', axis=1, tiled=True)]
    all_to_all x0 -> x1, waiting for transfers between devices: none -> 27 us  [local(): blocks = lax.all_to_all(blocks, 'col', split_axis=0, concat_axis=0)]
where the time goes in v1:
time: 1060 us
  waiting for transfers between devices  934 us (88%)
  matrix products  55.3 us (5%)
  local copies, waits for them, and re-layouts  30 us (3%)
  blocking collectives  16.4 us (2%)
  between operations  14.9 us (1%)
    psum x1, waiting for transfers between devices, local(): lax.psum(weight_part * float(node_total) ** (-0.5), ('row', 'col'))  722 us
    reduce_scatter x1, waiting for transfers between devices, local(): lax.psum_scatter(partial_value, 'col', scatter_dimension=1, tiled=True)  87.3 us
    reduce_scatter x1, waiting for transfers between devices, local(): lax.psum_scatter(partial_back, 'row', scatter_dimension=1, tiled=True)  32.7 us
    reduce_scatter x1, waiting for transfers between devices, local(): lax.psum_scatter(lax.dot_general(own_rows, features, (((0,), (0,)), ((),...  30.2 us
    all_to_all x1, waiting for transfers between devices, local(): blocks = lax.all_to_all(blocks, 'col', split_axis=0, concat_axis=0)  27 us
    dot_general x1, matrix products, tile_terms(): jnp.einsum('fgb,gab->fga', picked, chosen, precision=lax.Precision.HIGHEST)  24.3 us
    reduce_scatter x1, waiting for transfers between devices, local(): lax.psum_scatter(jnp.dot(own_cols, grad_mixed, preferred_element_type=jnp...  23.8 us
  transfers between devices with their start and end apart: 7, of which 7 were waited for; matrix products, arithmetic and copies ran while one was open for 2% of the time, Pallas kernels for 0%

profile of v1, /device:TPU:2, one launch (start us, length us, event | category | flops | bytes accessed | tf_op | source)
XLA Modules:
  0.0 1057.5 jit_solution(11824711245378906094)
XLA Ops:
  7.2 0.9 copy-done
  8.1 2.3 fusion.39
  10.5 30.2 %reduce-scatter.5.cloned.1.call-done = f32[64,512]{1,0:T(8,128)} async-done(((f32[256,512]{1,0:T(8,128)}), f32[64,512]{1,0:T(8,128)}) %reduce-scatter.5.cloned.1.call-update) | async-done | bytes 131088 | tf_op jit(solution)/shard_map/reduce_scatter | solution.py:46
  41.4 0.7 compare_select_fusion.2
  42.1 14.1 %gather_fusion = f32[160,128,128]{2,1,0:T(8,128)} fusion(f32[160,128,128]{2,1,0:T(8,128)} %param.15, s32[1024]{0:T(1024)S(1)} %pad_clamp_fusion.2), kind=kCustom, calls=%fused_computation.clone | custom fusion | bytes 20972160 | tf_op jit(solution)/shard_map/jit(_take)/gather | solution.py:12
  56.3 10.5 all-gather.2.cloned.1.call-done
  66.9 1.3 copy_bitcast_fusion.2
  68.2 3.3 gather_fusion.1
  71.5 24.3 %fusion.20 = f32[64,160,128]{2,0,1:T(8,128)S(1)} fusion(f32[160,64,128]{2,1,0:T(8,128)} %gather_fusion.1, pred[160]{0:T(512)(128)(4,1)S(1)} %get-tuple-element.7, f32[160,128,128]{2,1,0:T(8,128)} %gather_fusion, pred[160]{0:T(512)(128)(4,1)S(1)} %get-tuple-element.8), kind=kOutput, calls=%fused_computation.23 | convolution fusion | flops 2017198080 | bytes 20971840 | tf_op jit(solution)/shard_map/fgb,gab->fga/dot_general | solution.py:16
  95.8 5.6 fusion.8
  101.4 1.6 copy.29
  103.1 87.3 %reduce-scatter.7.cloned.1.call-done = f32[64,512]{1,0:T(8,128)} async-done(((f32[64,4096]{1,0:T(8,128)}), f32[64,512]{1,0:T(8,128)}) %reduce-scatter.7.cloned.1.call-update) | async-done | bytes 131088 | tf_op jit(solution)/shard_map/reduce_scatter | solution.py:62
  190.4 1.7 fusion.36
  192.0 1.1 stack.2
  193.1 4.5 all-to-all-start
  197.7 27.0 %all-to-all-done = f32[8,64,512]{2,1,0:T(8,128)S(1)} async-done(((f32[8,64,512]{2,1,0:T(8,128)}), f32[8,64,512]{2,1,0:T(8,128)S(1)}, u32[]{:S(2)}, u32[]{:S(2)}) %all-to-all-start) | async-done | bytes 1048608 | tf_op jit(solution)/shard_map/all_to_all | solution.py:67
  224.6 0.6 copy.15
  225.2 0.1 reshape_reshape.3
  225.3 0.6 copy.16
  225.9 3.3 gather_fusion.2
  229.2 13.9 %fusion.25 = f32[64,160,128]{2,0,1:T(8,128)S(1)} fusion(f32[160,64,128]{2,1,0:T(8,128)} %gather_fusion.2, pred[160]{0:T(512)(128)(4,1)S(1)} %compare_and_fusion, f32[160,128,128]{2,1,0:T(8,128)} %gather_fusion, pred[160]{0:T(512)(128)(4,1)S(1)} %get-tuple-element.8), kind=kOutput, calls=%fused_computation.24 | convolution fusion | flops 2017198080 | bytes 20971840 | tf_op jit(solution)/shard_map/fga,gab->fgb/dot_general | solution.py:14
  243.1 5.6 fusion.6
  248.7 1.6 copy.28
  250.3 0.0 all-reduce.2.cloned.1.call-start
  250.4 32.7 %reduce-scatter.9.cloned.1.call-done = f32[64,512]{1,0:T(8,128)} async-done(((f32[64,4096]{1,0:T(8,128)}), f32[64,512]{1,0:T(8,128)}) %reduce-scatter.9.cloned.1.call-update) | async-done | bytes 131088 | tf_op jit(solution)/shard_map/reduce_scatter | solution.py:72
  283.0 16.4 %all_gather.7 = f32[256,512]{1,0:T(8,128)S(1)} all-gather(f32[64,512]{1,0:T(8,128)} %reduce-scatter.9.cloned.1.call-done), channel_id=1, replica_groups=mesh['row'=8,'col'=8,'rep'=4] {'rep'}, dimensions={0}, use_global_device_ids=true | all-gather | bytes 655360 | tf_op jit(solution)/shard_map/all_gather | solution.py:86
  299.4 1.2 fusion.30
  300.7 0.0 reduce-scatter.11.cloned.1.call-start
  300.7 2.3 fusion.37
  303.1 722.3 %all-reduce.2.cloned.1.call-done = f32[64,256]{1,0:T(8,128)} async-done(((f32[64,256]{1,0:T(8,128)}), f32[64,256]{1,0:T(8,128)}) %all-reduce.2.cloned.1.call-update) | async-done | bytes 65552 | tf_op jit(solution)/shard_map/psum | solution.py:92
  1025.4 23.8 %reduce-scatter.11.cloned.1.call-done = f32[64,512]{1,0:T(8,128)} async-done(((f32[256,512]{1,0:T(8,128)}), f32[64,512]{1,0:T(8,128)}) %reduce-scatter.11.cloned.1.call-update) | async-done | bytes 131088 | tf_op jit(solution)/shard_map/reduce_scatter | solution.py:73
  1049.1 1.5 copy.32
  (29 shorter events, 0.3 us)
Async XLA Ops:
  7.2 1.0 copy-start
  7.2 33.5 %reduce-scatter.5.cloned.1.call-start = ((), (), s32[]{:S(2)}) async-start(), calls=%async_computation.5 | async-start | bytes 655360 | tf_op jit(solution)/shard_map/reduce_scatter | solution.py:46
  10.5 56.4 %all-gather.2.cloned.1.call-start = ((), (), s32[]{:S(2)}) async-start(), calls=%async_computation.6 | async-start | bytes 1179648 | tf_op jit(solution)/shard_map/all_gather | solution.py:58
  40.7 149.6 %reduce-scatter.7.cloned.1.call-start = ((), (), s32[]{:S(2)}) async-start(), calls=%async_computation.7 | async-start | bytes 1179648 | tf_op jit(solution)/shard_map/reduce_scatter | solution.py:62
  42.1 14.2 %copy-start.3 = (s32[160]{0:T(256)S(1)}, s32[160]{0:T(256)}, u32[]{:S(2)}) copy-start(s32[160]{0:T(256)} %param.17) | copy-start | bytes 1924
  42.1 14.2 %copy-start.5 = (s32[160]{0:T(256)S(1)}, s32[160]{0:T(256)}, u32[]{:S(2)}) copy-start(s32[160]{0:T(256)} %param.18) | copy-start | bytes 1924
  71.5 24.3 %copy-start.4 = (s32[160]{0:T(256)S(1)}, s32[160]{0:T(256)}, u32[]{:S(2)}) copy-start(s32[160]{0:T(256)} %param.16) | copy-start | bytes 1924
  95.8 94.6 %copy-start.2 = (f32[64,512]{1,0:T(8,128)S(1)}, f32[64,512]{1,0:T(8,128)}, u32[]{:S(2)}) copy-start(f32[64,512]{1,0:T(8,128)} %param.14) | copy-start | bytes 393220
  193.1 31.5 %all-to-all-start = ((f32[8,64,512]{2,1,0:T(8,128)}), f32[8,64,512]{2,1,0:T(8,128)S(1)}, u32[]{:S(2)}, u32[]{:S(2)}) async-start(f32[8,64,512]{2,1,0:T(8,128)} %stack.2), calls=%async_computation.2 | async-start | bytes 2097152 | tf_op jit(solution)/shard_map/all_to_all | solution.py:67
  197.6 85.4 %reduce-scatter.9.cloned.1.call-start = ((), (), s32[]{:S(2)}) async-start(), calls=%async_computation.8 | async-start | bytes 1179648 | tf_op jit(solution)/shard_map/reduce_scatter | solution.py:72
  243.1 56.4 %copy-start.1 = (f32[64,512]{1,0:T(8,128)S(1)}, f32[64,512]{1,0:T(8,128)}, u32[]{:S(2)}) copy-start(f32[64,512]{1,0:T(8,128)} %param.12) | copy-start | bytes 393220
  250.3 775.1 %all-reduce.2.cloned.1.call-start = ((), (), s32[]{:S(2)}) async-start(), calls=%async_computation.10 | async-start | bytes 131072 | tf_op jit(solution)/shard_map/psum | solution.py:92
  300.7 748.4 %reduce-scatter.11.cloned.1.call-start = ((), (), s32[]{:S(2)}) async-start(), calls=%async_computation.9 | async-start | bytes 655360 | tf_op jit(solution)/shard_map/reduce_scatter | solution.py:73
Sparse Core Ops, SparseCore 0:
  10.6 30.0 reduce-scatter.4
  42.5 24.2 all-gather.1
  103.2 87.1 reduce-scatter.6
  250.4 32.5 reduce-scatter.8
  300.8 724.5 all-reduce.1
  1028.3 20.7 reduce-scatter.10
